TPU v7x, 128 devices: a whole 4x4x4 slice. The times are simulated.
128 devices in a mesh: grp: 2 (over y_lo), tp: 64 (over y_hi, z, x, core).
Axes of the slice: x: 4, y: 4 (y_hi: 2, y_lo: 2; y = y_hi * 2 + y_lo), z: 4, core: 2. Of those that a mesh axis runs over, the one named last changes fastest.
Arguments:
- patches: bfloat16 [5120, 1408], P('tp'), may hold values from -6 to 6
- grids: int32 [64, 3, 2], P('tp'), may hold values from 0 to 40, as said below
- positions: int32 [1280], replicated, may hold values from 0 to 2048, as said below
- vis_gain: float32 [1408], replicated, may hold values from 0.1 to 1.9
- vis_query: bfloat16 [1408, 1408], P(None, 'grp')
- vis_key: bfloat16 [1408, 1408], P(None, 'grp'), may hold values from -0.15625 to 0.15625
- vis_value: bfloat16 [1408, 1408], P(None, 'grp'), may hold values from -0.15625 to 0.15625
- vis_out: bfloat16 [1408, 1408], P('grp'), may hold values from -0.15625 to 0.15625
- w_proj: bfloat16 [5632, 4096], P(None, 'tp'), may hold values from -0.078125 to 0.078125
- text_embed: bfloat16 [2048, 4096], P(('grp', 'tp')), may hold values from -6 to 6
- slots: int32 [2, 512], P('grp'), may hold values from 0 to 1023, as said below
- lengths: int32 [2, 8], P('grp'), may hold values from 1 to 256, 1024 in all within a row
- attn_gain: float32 [4096], replicated, may hold values from 0.1 to 1.9
- mlp_gain: float32 [4096], replicated, may hold values from 0.1 to 1.9
- w_kv: bfloat16 [4096, 8192], P(None, 'tp'), may hold values from -0.09375 to 0.09375
- w_gate: bfloat16 [4096, 11008], P(None, 'tp'), may hold values from -0.09375 to 0.09375
- w_up: bfloat16 [4096, 11008], P(None, 'tp'), may hold values from -0.09375 to 0.09375
- w_down: bfloat16 [11008, 4096], P('tp'), may hold values from -0.0546875 to 0.0546875
Outputs:
- layer_out: bfloat16 [2048, 4096], P(('grp', 'tp'))
- kv_out: bfloat16 [2, 512, 8192], P('grp', None, 'tp')
Inputs may be any that keep to these rules, and one draw needn't show every extreme that they name: `grids`: heights and widths are even; the areas of one tp index sum to at most 80; a height of 0 marks an empty entry. `positions`: every merged cell slot inside an image holds a distinct prompt position below 2048, increasing with the slot; slots past a block's images hold 2048. `slots`: distinct within each batch.
All inputs are finite; a program needn't handle non-finite values.
Results may differ from a plain program's by a relative error of at most 0.014.
The roundings to bfloat16 on the way count: a program that leaves them out, or rounds other values in their place, can miss the bound.
Values may be sent and summed in bfloat16 or wider, within the bound.
A program may use at most 128 MiB of HBM per device.

v0:
```python
import math
import jax
import jax.numpy as jnp
from jax import lax
from jax.sharding import PartitionSpec as P

VHD = 88
HD = 128
PATCH_DEV = 80
MERGE_DEV = 20
IMGS = 3


def layer_norm(row_data, gain_vec):
    as_float = row_data.astype(jnp.float32)
    center = as_float - jnp.mean(as_float, axis=-1, keepdims=True)
    spread = jnp.mean(center * center, axis=-1, keepdims=True)
    return (center * lax.rsqrt(spread + 1e-06) * gain_vec).astype(jnp.bfloat16)


def rms_norm(row_data, gain_vec):
    as_float = row_data.astype(jnp.float32)
    square_mean = jnp.mean(as_float * as_float, axis=-1, keepdims=True)
    return (as_float * lax.rsqrt(square_mean + 1e-05) * gain_vec).astype(jnp.bfloat16)


def image_tables(grid_dev):
    heights = grid_dev[:, 0]
    widths = grid_dev[:, 1]
    areas = heights * widths
    seg_ends = jnp.cumsum(areas)
    slot_ids = jnp.arange(PATCH_DEV, dtype=jnp.int32)
    segment = jnp.sum((slot_ids[:, None] >= seg_ends[None, :]).astype(jnp.int32), axis=1)
    cell_areas = areas // 4
    cell_ends = jnp.cumsum(cell_areas)
    cell_starts = cell_ends - cell_areas
    cell_ids = jnp.arange(MERGE_DEV, dtype=jnp.int32)
    which = jnp.sum((cell_ids[:, None] >= cell_ends[None, :]).astype(jnp.int32), axis=1)
    which = jnp.minimum(which, IMGS - 1)
    select = (which[:, None] == jnp.arange(IMGS, dtype=jnp.int32)[None, :]).astype(jnp.int32)
    start_cell = jnp.sum(select * cell_starts[None, :], axis=1)
    width_sel = jnp.sum(select * widths[None, :], axis=1)
    half_width = jnp.maximum(width_sel // 2, 1)
    inner = cell_ids - start_cell
    row_pair = inner // half_width
    col_pair = inner % half_width
    corner = 4 * start_cell + 2 * row_pair * width_sel + 2 * col_pair
    corners = jnp.stack([corner, corner + 1, corner + width_sel, corner + width_sel + 1], axis=1)
    valid = cell_ids < cell_ends[IMGS - 1]
    return (segment, jnp.where(valid[:, None], corners, 0))


def rotate_keys(values_f, token_pos, first_col):
    col_count = values_f.shape[1]
    col_ids = first_col + jnp.arange(0, col_count, 2, dtype=jnp.int32)
    pair_ids = col_ids % HD // 2
    is_key = col_ids // HD % 2 == 0
    freq = jnp.exp(pair_ids.astype(jnp.float32) * (-2.0 * math.log(10000.0) / HD))
    angle = token_pos.astype(jnp.float32)[:, None] * freq[None, :]
    cosine = jnp.where(is_key[None, :], jnp.cos(angle), 1.0)
    sine = jnp.where(is_key[None, :], jnp.sin(angle), 0.0)
    paired = values_f.reshape(values_f.shape[0], col_count // 2, 2)
    even_part = paired[:, :, 0]
    odd_part = paired[:, :, 1]
    turned = jnp.stack(
        [even_part * cosine - odd_part * sine, even_part * sine + odd_part * cosine], axis=2
    )
    return turned.reshape(values_f.shape[0], col_count)


def slot_positions(slot_ids, length_row):
    req_ends = jnp.cumsum(length_row)
    req_starts = req_ends - length_row
    inside = (slot_ids[:, None] >= req_starts[None, :]) & (slot_ids[:, None] < req_ends[None, :])
    return slot_ids - jnp.sum(jnp.where(inside, req_starts[None, :], 0), axis=1)


def local(
    patches,
    grids,
    positions,
    vis_gain,
    vis_query,
    vis_key,
    vis_value,
    vis_out,
    w_proj,
    text_embed,
    slots,
    lengths,
    attn_gain,
    mlp_gain,
    w_kv,
    w_gate,
    w_up,
    w_down,
):
    segment, corners = image_tables(grids[0])
    normed = layer_norm(patches, vis_gain)
    query_rows = jnp.dot(normed, vis_query, preferred_element_type=jnp.float32).astype(jnp.bfloat16)
    key_rows = jnp.dot(normed, vis_key, preferred_element_type=jnp.float32).astype(jnp.bfloat16)
    value_rows = jnp.dot(normed, vis_value, preferred_element_type=jnp.float32).astype(jnp.bfloat16)
    slot_count = patches.shape[0]
    head_count = query_rows.shape[1] // VHD
    head_query = query_rows.reshape(slot_count, head_count, VHD)
    head_key = key_rows.reshape(slot_count, head_count, VHD)
    head_value = value_rows.reshape(slot_count, head_count, VHD)
    scores = jnp.einsum(
        "qhd,khd->hqk", head_query, head_key, preferred_element_type=jnp.float32
    ) * VHD ** (-0.5)
    allowed = segment[:, None] == segment[None, :]
    scores = jnp.where(allowed[None, :, :], scores, -1e30)
    row_max = jnp.max(scores, axis=-1, keepdims=True)
    expos = jnp.exp(scores - row_max)
    attn_probs = (expos / jnp.sum(expos, axis=-1, keepdims=True)).astype(jnp.bfloat16)
    context = jnp.einsum("hqk,khd->qhd", attn_probs, head_value, preferred_element_type=jnp.float32)
    context = context.reshape(slot_count, head_count * VHD).astype(jnp.bfloat16)
    partial_out = jnp.dot(context, vis_out, preferred_element_type=jnp.float32)
    attended = lax.psum(partial_out.astype(jnp.bfloat16), "grp").astype(jnp.float32)
    vision = (patches.astype(jnp.float32) + attended).astype(jnp.bfloat16)
    merged = vision[corners.reshape(-1)].reshape(corners.shape[0], 4 * patches.shape[1])
    tok_dev = text_embed.shape[0]
    tp_count = lax.axis_size("tp")
    half_tok = tok_dev * tp_count
    group_index = lax.axis_index("grp")
    tp_index = lax.axis_index("tp")
    col_count = w_proj.shape[1]
    image_cols = jnp.dot(
        lax.all_gather(merged, "tp", axis=0, tiled=True), w_proj, preferred_element_type=jnp.float32
    ).astype(jnp.bfloat16)
    local_rows = positions - group_index * half_tok
    inside = (local_rows >= 0) & (local_rows < half_tok)
    local_rows = jnp.where(inside, local_rows, half_tok)
    buffer = (
        jnp.zeros((half_tok, col_count), jnp.bfloat16).at[local_rows].set(image_cols, mode="drop")
    )
    placed = lax.all_to_all(buffer, "tp", split_axis=0, concat_axis=1, tiled=True)
    first_row = (group_index * tp_count + tp_index) * tok_dev
    own_rows = first_row + jnp.arange(tok_dev, dtype=jnp.int32)
    is_image = jnp.any(positions[None, :] == own_rows[:, None], axis=1)
    assembled = jnp.where(is_image[:, None], placed, text_embed)
    token_batch = lax.all_gather(assembled, "tp", axis=0, tiled=True)
    mlp_normed = rms_norm(token_batch, mlp_gain)
    gate_val = jnp.dot(mlp_normed, w_gate, preferred_element_type=jnp.float32)
    up_val = jnp.dot(mlp_normed, w_up, preferred_element_type=jnp.float32)
    hidden = (jax.nn.silu(gate_val) * up_val).astype(jnp.bfloat16)
    every_term = jnp.dot(hidden, w_down, preferred_element_type=jnp.float32)
    every_sum = lax.psum(every_term, "tp")
    mixed = lax.dynamic_slice_in_dim(every_sum, tp_index * tok_dev, tok_dev, 0)
    layer_out = (assembled.astype(jnp.float32) + mixed).astype(jnp.bfloat16)
    slot_ids = slots[0]
    slot_rows = token_batch[slot_ids]
    attn_normed = rms_norm(slot_rows, attn_gain)
    kv_cols = jnp.dot(attn_normed, w_kv, preferred_element_type=jnp.float32)
    token_pos = slot_positions(slot_ids, lengths[0])
    kv_out = rotate_keys(kv_cols, token_pos, tp_index * w_kv.shape[1]).astype(jnp.bfloat16)
    return (layer_out, kv_out[None])


def solution(mesh):
    return jax.shard_map(
        local,
        mesh=mesh,
        in_specs=(
            P("tp", None),
            P("tp", None, None),
            P(),
            P(),
            P(None, "grp"),
            P(None, "grp"),
            P(None, "grp"),
            P("grp", None),
            P(None, "tp"),
            P(("grp", "tp"), None),
            P("grp", None),
            P("grp", None),
            P(),
            P(),
            P(None, "tp"),
            P(None, "tp"),
            P(None, "tp"),
            P("tp", None),
        ),
        out_specs=(P(("grp", "tp"), None), P("grp", None, "tp")),
        check_vma=False,
    )
```

profile of v0, /device:TPU:1, one launch (start us, length us, event | category | flops | bytes accessed | tf_op | source)
XLA Modules:
  0.0 1008.9 jit_solution(15142676936785822267)
XLA Ops:
  7.3 1.2 convert_reduce_fusion
  8.5 1.2 fusion.35
  9.7 0.8 and_select_fusion.8
  10.4 0.2 reduce-window.18
  10.8 2.4 convolution_convert_fusion.4
  13.2 0.2 reshape.622
  13.5 2.4 convolution_convert_fusion.3
  15.9 0.2 reshape.623
  16.1 0.2 fusion.25
  16.4 2.4 convolution_convert_fusion.5
  18.9 0.2 reshape.620
  19.1 0.3 fusion.27
  19.6 1.2 convolution_convert_fusion
  20.8 0.2 reduce-window.19
  21.0 0.6 slice.18
  21.6 0.7 iota_compare_fusion.3
  22.9 30.2 %all-reduce.3.cloned.1.call-done = bf16[80,1408]{1,0:T(8,128)(2,1)} async-done(((bf16[80,1408]{1,0:T(8,128)(2,1)}), bf16[80,1408]{1,0:T(8,128)(2,1)}) %all-reduce.3.cloned.1.call-update) | async-done | bytes 225296 | tf_op jit(solution)/shard_map/psum | solution.py:119
  53.0 1.0 fusion.38
  54.0 0.8 gather_fusion
  54.8 0.9 reshape.653
  55.7 110.1 %all-gather.6.cloned.1.call-done = bf16[64,20,5632]{2,1,0:T(8,128)(2,1)} async-done(((bf16[1,20,5632]{2,1,0:T(8,128)(2,1)}), bf16[64,20,5632]{2,1,0:T(8,128)(2,1)}) %all-gather.6.cloned.1.call-update) | async-done | bytes 14417936 | tf_op jit(solution)/shard_map/all_gather | solution.py:129
  165.9 17.6 %reshape.654 = bf16[1280,5632]{1,0:T(8,128)(2,1)} reshape(bf16[64,20,5632]{2,1,0:T(8,128)(2,1)} %all-gather.6.cloned.1.call-done) | data formatting | bytes 28835840
  183.4 9.6 convolution_convert_fusion.1
  193.0 0.2 copy.50
  193.2 6.3 scatter_custom_fusion
  199.5 0.8 reshape.658
  200.4 5.9 all-to-all-start
  206.3 0.2 compare_reduce_fusion
  206.5 9.8 all-to-all-done
  216.3 0.2 reshape.659
  216.6 0.3 all_to_all.17
  216.9 0.7 broadcast_select_fusion.2
  217.6 0.2 all-reduce.5.cloned.1.call-start
  217.9 77.9 %all-gather.4.cloned.1.call-done = bf16[1024,4096]{1,0:T(8,128)(2,1)} async-done(((bf16[16,4096]{1,0:T(8,128)(2,1)}), bf16[1024,4096]{1,0:T(8,128)(2,1)}) %all-gather.4.cloned.1.call-update) | async-done | bytes 8388624 | tf_op jit(solution)/shard_map/all_gather | solution.py:142
  295.8 5.2 fusion.1
  301.0 0.5 copy-done.2
  301.6 4.7 fusion.13
  306.3 11.7 %fusion.22 = f32[1024,4096]{1,0:T(8,128)} fusion(bf16[172,4096]{1,0:T(8,128)(2,1)} %param.35, bf16[4096,172]{0,1:T(8,128)(2,1)S(1)} %copy-done.4, bf16[1024,4096]{1,0:T(8,128)(2,1)} %all-gather.4.cloned.1.call-done, f32[4096]{0:T(1024)S(1)} %copy-done.8, f32[1024]{0:T(1024)S(1)} %add_rsqrt_fusion, f32[1024,172]{0,1:T(8,128)S(1)} %fusion.13), kind=kOutput, calls=%fused_computation.23 | convolution fusion | flops 2903515136 | bytes 28708864 | tf_op jit(solution)/shard_map/dot_general | solution.py:147
  318.1 0.6 copy-done.13
  318.7 0.2 reduce-window.20
  319.1 13.0 %gather_fusion.1 = bf16[512,4096]{1,0:T(8,128)(2,1)} fusion(bf16[1024,4096]{1,0:T(8,128)(2,1)} %all-gather.4.cloned.1.call-done, s32[1024]{0:T(1024)S(1)} %pad_clamp_fusion), kind=kCustom, calls=%fused_computation.1 | custom fusion | bytes 8390656 | tf_op jit(solution)/shard_map/gather | solution.py:152
  332.1 3.2 fusion.4
  335.4 4.2 fusion.7
  339.7 4.5 subtract_convert_fusion
  344.2 0.3 pad_maximum_fusion
  344.6 0.8 copy.52
  345.3 655.4 %all-reduce.5.cloned.1.call-done = f32[1024,4096]{1,0:T(8,128)} async-done(((f32[1024,4096]{1,0:T(8,128)}), f32[1024,4096]{1,0:T(8,128)}) %all-reduce.5.cloned.1.call-update) | async-done | bytes 16777232 | tf_op jit(solution)/shard_map/psum | solution.py:148
  1000.7 1.6 add_convert_fusion
  (65 shorter events, 1.7 us)
Async XLA Ops:
  7.2 12.4 %copy-start = (bf16[704,1408]{1,0:T(8,128)(2,1)S(1)}, bf16[704,1408]{1,0:T(8,128)(2,1)}, u32[]{:S(2)}) copy-start(bf16[704,1408]{1,0:T(8,128)(2,1)} %param.25) | copy-start | bytes 5947396
  7.2 45.9 %copy-start.3 = (bf16[80,1408]{1,0:T(8,128)(2,1)S(1)}, bf16[80,1408]{1,0:T(8,128)(2,1)}, u32[]{:S(2)}) copy-start(bf16[80,1408]{1,0:T(8,128)(2,1)} %param.18) | copy-start | bytes 675844
  7.2 14.4 %copy-start.11 = (s32[1,3,2]{1,2,0:T(2,128)S(1)}, s32[1,3,2]{1,2,0:T(2,128)}, u32[]{:S(2)}) copy-start(s32[1,3,2]{1,2,0:T(2,128)} %param.19) | copy-start | bytes 76
  7.2 45.8 %all-reduce.3.cloned.1.call-start = ((), (), s32[]{:S(2)}) async-start(), calls=%async_computation.1 | async-start | bytes 450560 | tf_op jit(solution)/shard_map/psum | solution.py:119
  10.8 44.9 %copy-start.9 = (s32[1280]{0:T(1024)S(1)}, s32[1280]{0:T(1024)}, u32[]{:S(2)}) copy-start(s32[1280]{0:T(1024)} %param.20) | copy-start | bytes 15364
  20.8 145.1 %all-gather.6.cloned.1.call-start = ((), (), s32[]{:S(2)}) async-start(), calls=%async_computation.4 | async-start | bytes 17571840 | tf_op jit(solution)/shard_map/all_gather | solution.py:129
  55.7 127.7 %copy-start.6 = (bf16[5632,64]{0,1:T(8,128)(2,1)S(1)}, bf16[5632,64]{0,1:T(8,128)(2,1)}, u32[]{:S(2)}) copy-start(bf16[5632,64]{0,1:T(8,128)(2,1)} %param.26) | copy-start | bytes 2162692
  183.4 33.5 %copy-start.7 = (bf16[16,4096]{1,0:T(8,128)(2,1)S(1)}, bf16[16,4096]{1,0:T(8,128)(2,1)}, u32[]{:S(2)}) copy-start(bf16[16,4096]{1,0:T(8,128)(2,1)} %param.27) | copy-start | bytes 393220
  193.0 108.1 %copy-start.8 = (f32[4096]{0:T(1024)S(1)}, f32[4096]{0:T(1024)}, u32[]{:S(2)}) copy-start(f32[4096]{0:T(1024)} %param.31) | copy-start | bytes 49156
  200.4 15.9 %all-to-all-start = ((bf16[64,2,512]{2,1,0:T(2,128)(2,1)}), bf16[64,2,512]{2,1,0:T(2,128)(2,1)S(1)}, u32[]{:S(2)}, u32[]{:S(2)}) async-start(bf16[64,2,512]{2,1,0:T(2,128)(2,1)} %reshape.658), calls=%async_computation | async-start | bytes 262144 | tf_op jit(solution)/shard_map/all_to_all | solution.py:137
  206.3 89.5 %all-gather.4.cloned.1.call-start = ((), (), s32[]{:S(2)}) async-start(), calls=%async_computation.2 | async-start | bytes 8519680 | tf_op jit(solution)/shard_map/all_gather | solution.py:142
  217.6 783.1 %all-reduce.5.cloned.1.call-start = ((), (), s32[]{:S(2)}) async-start(), calls=%async_computation.3 | async-start | bytes 33554432 | tf_op jit(solution)/shard_map/psum | solution.py:148
  295.8 5.8 copy-start.2
  301.6 4.7 copy-start.4
  318.0 0.7 copy-start.13
  318.0 0.9 copy-start.10
  319.1 16.3 %copy-start.12 = (f32[4096]{0:T(1024)S(1)}, f32[4096]{0:T(1024)}, u32[]{:S(2)}) copy-start(f32[4096]{0:T(1024)} %param.30) | copy-start | bytes 49156
  332.1 668.6 %copy-start.5 = (bf16[16,4096]{1,0:T(8,128)(2,1)S(1)}, bf16[16,4096]{1,0:T(8,128)(2,1)}, u32[]{:S(2)}) copy-start(bf16[16,4096]{1,0:T(8,128)(2,1)} %broadcast_select_fusion.2) | copy-start | bytes 393220
  332.1 670.3 %copy-start.1 = (bf16[704,1408]{1,0:T(8,128)(2,1)S(1)}, bf16[704,1408]{1,0:T(8,128)(2,1)}, u32[]{:S(2)}) copy-start(bf16[704,1408]{1,0:T(8,128)(2,1)} %param.25) | copy-start | bytes 5947396
Sparse Core Ops, SparseCore 0:
  20.9 32.0 all-reduce.2
  56.3 109.4 all-gather.5
  217.8 77.9 all-gather.3
  318.2 682.4 all-reduce.4
where the time goes:
time: 1010 us
  waiting for transfers between devices  883 us (87%)
  local copies, waits for them, and re-layouts  43.9 us (4%)
  matrix products  39.2 us (4%)
  other arithmetic  21.9 us (2%)
  between operations  14.2 us (1%)
    psum x1, waiting for transfers between devices, local(): every_sum = lax.psum(every_term, 'tp')  655 us
    all_gather x1, waiting for transfers between devices, local(): lax.all_gather(merged, 'tp', axis=0, tiled=True)  110 us
    all_gather x1, waiting for transfers between devices, local(): token_batch = lax.all_gather(assembled, 'tp', axis=0, tiled=True)  77.9 us
    psum x1, waiting for transfers between devices, local(): lax.psum(partial_out.astype(jnp.bfloat16), 'grp').astype(jnp.float32)  30.2 us
    unnamed x33, local copies, waits for them, and re-layouts  21.5 us
  transfers between devices with their start and end apart: 5, of which 5 were waited for; matrix products, arithmetic and copies ran while one was open for 3% of the time, Pallas kernels for 0%

commit v1 on v0

--- a/solution.py
+++ b/solution.py
@@ -3,6 +3,7 @@
 import jax.numpy as jnp
 from jax import lax
 from jax.sharding import PartitionSpec as P
+from jax.lax import all_to_all, axis_size
 
 VHD = 88
 HD = 128
@@ -126,7 +127,17 @@
     tp_index = lax.axis_index("tp")
     col_count = w_proj.shape[1]
     image_cols = jnp.dot(
-        lax.all_gather(merged, "tp", axis=0, tiled=True), w_proj, preferred_element_type=jnp.float32
+        jnp.concatenate(
+            all_to_all(
+                jnp.stack([merged for _ in range(axis_size("tp"))], 0),
+                concat_axis=0,
+                split_axis=0,
+                axis_name="tp",
+            ),
+            0,
+        ),
+        w_proj,
+        preferred_element_type=jnp.float32,
     ).astype(jnp.bfloat16)
     local_rows = positions - group_index * half_tok
     inside = (local_rows >= 0) & (local_rows < half_tok)

time: 1010 us -> 1170 us (1.16)
  waiting for transfers between devices: 883 us -> 1020 us
  starting transfers between devices: 6.23 us -> 30.1 us
    all_to_all x0 -> x1, waiting for transfers between devices: none -> 245 us  [local(): all_to_all(jnp.stack([merged for _ in range(axis_size('tp'))], 0), concat...]
    all_gather x1 -> x0, waiting for transfers between devices: 110 us -> none  [local(): lax.all_gather(merged, 'tp', axis=0, tiled=True)]
    unnamed x33 -> x31, local copies, waits for them, and re-layouts: 21.5 us -> 3.03 us
    reshape x0 -> x1, local copies, waits for them, and re-layouts: none -> 17.6 us  [local(): jnp.concatenate(all_to_all(jnp.stack([merged for _ in range(axis_size('tp...]
    all_to_all x1, starting transfers between devices: 5.88 us -> 18.8 us  [local(): lax.all_to_all(buffer, 'tp', split_axis=0, concat_axis=1, tiled=True)]
  transfers between devices with their start and end apart: 5 -> 5, of which waited for: 5 -> 5; matrix products, arithmetic and copies ran while one was open for 3% -> 2% of each run, Pallas kernels for 0% -> 0%
where the time goes in v1:
time: 1170 us
  waiting for transfers between devices  1020 us (87%)
  local copies, waits for them, and re-layouts  49.4 us (4%)
  matrix products  39.2 us (3%)
  starting transfers between devices  30.1 us (3%)
  other arithmetic  21.9 us (2%)
  between operations  14.2 us (1%)
    psum x1, waiting for transfers between devices, local(): every_sum = lax.psum(every_term, 'tp')  655 us
    all_to_all x1, waiting for transfers between devices, local(): all_to_all(jnp.stack([merged for _ in range(axis_size('tp'))], 0), concat...  245 us
    all_gather x1, waiting for transfers between devices, local(): token_batch = lax.all_gather(assembled, 'tp', axis=0, tiled=True)  77.1 us
    psum x1, waiting for transfers between devices, local(): lax.psum(partial_out.astype(jnp.bfloat16), 'grp').astype(jnp.float32)  30.2 us
  transfers between devices with their start and end apart: 5, of which 5 were waited for; matrix products, arithmetic and copies ran while one was open for 2% of the time, Pallas kernels for 0%

profile of v1, /device:TPU:1, one launch (start us, length us, event | category | flops | bytes accessed | tf_op | source)
XLA Modules:
  0.0 1171.6 jit_solution(6493756852267856910)
XLA Ops:
  7.2 0.8 and_select_fusion.8
  8.1 1.1 convert_reduce_fusion
  9.2 1.2 fusion.35
  10.4 2.4 convolution_convert_fusion.4
  12.8 0.2 reshape.624
  13.0 2.4 convolution_convert_fusion.3
  15.5 0.2 reshape.625
  15.7 0.2 reduce-window.18
  16.0 0.2 fusion.25
  16.4 2.4 convolution_convert_fusion.5
  18.8 0.2 reshape.622
  19.0 0.3 fusion.27
  19.5 1.2 convolution_convert_fusion
  20.9 0.6 slice.18
  21.8 0.7 iota_compare_fusion.3
  22.7 30.2 %all-reduce.3.cloned.1.call-done = bf16[80,1408]{1,0:T(8,128)(2,1)} async-done(((bf16[80,1408]{1,0:T(8,128)(2,1)}), bf16[80,1408]{1,0:T(8,128)(2,1)}) %all-reduce.3.cloned.1.call-update) | async-done | bytes 225296 | tf_op jit(solution)/shard_map/psum | solution.py:120
  53.0 1.0 fusion.38
  54.0 0.8 gather_fusion
  54.9 6.2 stack.8
  61.1 10.9 all-to-all-start
  72.1 244.5 %all-to-all-done = bf16[64,20,5632]{2,1,0:T(8,128)(2,1)} async-done(((bf16[64,20,5632]{2,1,0:T(8,128)(2,1)}), bf16[64,20,5632]{2,1,0:T(8,128)(2,1)}, u32[]{:S(2)}, u32[]{:S(2)}) %all-to-all-start) | async-done | bytes 14417952 | tf_op jit(solution)/shard_map/all_to_all | solution.py:131
  316.6 17.6 %reshape.626 = bf16[1280,5632]{1,0:T(8,128)(2,1)} reshape(bf16[64,20,5632]{2,1,0:T(8,128)(2,1)} %all-to-all-done) | data formatting | bytes 28835840 | tf_op jit(solution)/shard_map/reshape | solution.py:130
  334.2 9.6 convolution_convert_fusion.1
  343.8 0.2 copy.41
  344.0 6.3 scatter_custom_fusion
  350.3 0.8 reshape.657
  351.1 18.8 %all-to-all-start.1 = ((bf16[64,2,512]{2,1,0:T(2,128)(2,1)}), bf16[64,2,512]{2,1,0:T(2,128)(2,1)S(1)}, u32[]{:S(2)}, u32[]{:S(2)}) async-start(bf16[64,2,512]{2,1,0:T(2,128)(2,1)} %reshape.657), calls=%async_computation.1 | async-start | bytes 262144 | tf_op jit(solution)/shard_map/all_to_all | solution.py:148
  370.0 0.2 compare_reduce_fusion
  370.2 9.8 all-to-all-done.1
  380.0 0.2 reshape.658
  380.3 0.3 all_to_all.21
  380.6 0.7 broadcast_select_fusion.2
  381.4 0.2 all-reduce.5.cloned.1.call-start
  381.6 77.1 %all-gather.2.cloned.1.call-done = bf16[1024,4096]{1,0:T(8,128)(2,1)} async-done(((bf16[16,4096]{1,0:T(8,128)(2,1)}), bf16[1024,4096]{1,0:T(8,128)(2,1)}) %all-gather.2.cloned.1.call-update) | async-done | bytes 8388624 | tf_op jit(solution)/shard_map/all_gather | solution.py:153
  458.7 5.2 fusion.1
  463.9 0.5 copy-done.2
  464.5 4.7 fusion.13
  469.2 11.7 %fusion.22 = f32[1024,4096]{1,0:T(8,128)} fusion(bf16[172,4096]{1,0:T(8,128)(2,1)} %param.35, bf16[4096,172]{0,1:T(8,128)(2,1)S(1)} %copy-done.4, bf16[1024,4096]{1,0:T(8,128)(2,1)} %all-gather.2.cloned.1.call-done, f32[4096]{0:T(1024)S(1)} %copy-done.8, f32[1024]{0:T(1024)S(1)} %add_rsqrt_fusion, f32[1024,172]{0,1:T(8,128)S(1)} %fusion.13), kind=kOutput, calls=%fused_computation.23 | convolution fusion | flops 2903515136 | bytes 28708864 | tf_op jit(solution)/shard_map/dot_general | solution.py:158
  481.0 0.6 copy-done.13
  481.6 0.2 reduce-window.20
  482.0 13.0 %gather_fusion.1 = bf16[512,4096]{1,0:T(8,128)(2,1)} fusion(bf16[1024,4096]{1,0:T(8,128)(2,1)} %all-gather.2.cloned.1.call-done, s32[1024]{0:T(1024)S(1)} %pad_clamp_fusion), kind=kCustom, calls=%fused_computation.1 | custom fusion | bytes 8390656 | tf_op jit(solution)/shard_map/gather | solution.py:163
  495.0 3.2 fusion.4
  498.2 4.2 fusion.7
  502.6 4.5 subtract_convert_fusion
  507.1 0.3 pad_maximum_fusion
  507.4 0.8 copy.43
  508.2 655.2 %all-reduce.5.cloned.1.call-done = f32[1024,4096]{1,0:T(8,128)} async-done(((f32[1024,4096]{1,0:T(8,128)}), f32[1024,4096]{1,0:T(8,128)}) %all-reduce.5.cloned.1.call-update) | async-done | bytes 16777232 | tf_op jit(solution)/shard_map/psum | solution.py:159
  1163.4 1.6 add_convert_fusion
  (65 shorter events, 2.0 us)
Async XLA Ops:
  7.2 12.4 %copy-start = (bf16[704,1408]{1,0:T(8,128)(2,1)S(1)}, bf16[704,1408]{1,0:T(8,128)(2,1)}, u32[]{:S(2)}) copy-start(bf16[704,1408]{1,0:T(8,128)(2,1)} %param.25) | copy-start | bytes 5947396
  7.2 13.7 %copy-start.11 = (s32[1,3,2]{1,2,0:T(2,128)S(1)}, s32[1,3,2]{1,2,0:T(2,128)}, u32[]{:S(2)}) copy-start(s32[1,3,2]{1,2,0:T(2,128)} %param.19) | copy-start | bytes 76
  7.2 45.8 %copy-start.3 = (bf16[80,1408]{1,0:T(8,128)(2,1)S(1)}, bf16[80,1408]{1,0:T(8,128)(2,1)}, u32[]{:S(2)}) copy-start(bf16[80,1408]{1,0:T(8,128)(2,1)} %param.18) | copy-start | bytes 675844
  7.2 45.8 %all-reduce.3.cloned.1.call-start = ((), (), s32[]{:S(2)}) async-start(), calls=%async_computation.2 | async-start | bytes 450560 | tf_op jit(solution)/shard_map/psum | solution.py:120
  61.1 11.0 copy-start.9
  61.1 255.5 %all-to-all-start = ((bf16[64,20,5632]{2,1,0:T(8,128)(2,1)}), bf16[64,20,5632]{2,1,0:T(8,128)(2,1)}, u32[]{:S(2)}, u32[]{:S(2)}) async-start(bf16[64,20,5632]{2,1,0:T(8,128)(2,1)} %stack.8), calls=%async_computation | async-start | bytes 34603008 | tf_op jit(solution)/shard_map/all_to_all | solution.py:131
  72.1 262.1 %copy-start.6 = (bf16[5632,64]{0,1:T(8,128)(2,1)S(1)}, bf16[5632,64]{0,1:T(8,128)(2,1)}, u32[]{:S(2)}) copy-start(bf16[5632,64]{0,1:T(8,128)(2,1)} %param.26) | copy-start | bytes 2162692
  334.2 46.4 %copy-start.7 = (bf16[16,4096]{1,0:T(8,128)(2,1)S(1)}, bf16[16,4096]{1,0:T(8,128)(2,1)}, u32[]{:S(2)}) copy-start(bf16[16,4096]{1,0:T(8,128)(2,1)} %param.27) | copy-start | bytes 393220
  343.8 120.2 %copy-start.8 = (f32[4096]{0:T(1024)S(1)}, f32[4096]{0:T(1024)}, u32[]{:S(2)}) copy-start(f32[4096]{0:T(1024)} %param.31) | copy-start | bytes 49156
  351.1 28.9 %all-to-all-start.1 = ((bf16[64,2,512]{2,1,0:T(2,128)(2,1)}), bf16[64,2,512]{2,1,0:T(2,128)(2,1)S(1)}, u32[]{:S(2)}, u32[]{:S(2)}) async-start(bf16[64,2,512]{2,1,0:T(2,128)(2,1)} %reshape.657), calls=%async_computation.1 | async-start | bytes 262144 | tf_op jit(solution)/shard_map/all_to_all | solution.py:148
  370.0 88.7 %all-gather.2.cloned.1.call-start = ((), (), s32[]{:S(2)}) async-start(), calls=%async_computation.3 | async-start | bytes 8519680 | tf_op jit(solution)/shard_map/all_gather | solution.py:153
  381.4 782.0 %all-reduce.5.cloned.1.call-start = ((), (), s32[]{:S(2)}) async-start(), calls=%async_computation.4 | async-start | bytes 33554432 | tf_op jit(solution)/shard_map/psum | solution.py:159
  458.7 5.8 copy-start.2
  464.5 4.7 copy-start.4
  480.9 0.7 copy-start.13
  480.9 0.9 copy-start.10
  482.0 16.3 %copy-start.12 = (f32[4096]{0:T(1024)S(1)}, f32[4096]{0:T(1024)}, u32[]{:S(2)}) copy-start(f32[4096]{0:T(1024)} %param.30) | copy-start | bytes 49156
  495.0 668.4 %copy-start.5 = (bf16[16,4096]{1,0:T(8,128)(2,1)S(1)}, bf16[16,4096]{1,0:T(8,128)(2,1)}, u32[]{:S(2)}) copy-start(bf16[16,4096]{1,0:T(8,128)(2,1)} %broadcast_select_fusion.2) | copy-start | bytes 393220
  495.0 670.1 %copy-start.1 = (bf16[704,1408]{1,0:T(8,128)(2,1)S(1)}, bf16[704,1408]{1,0:T(8,128)(2,1)}, u32[]{:S(2)}) copy-start(bf16[704,1408]{1,0:T(8,128)(2,1)} %param.25) | copy-start | bytes 5947396
Sparse Core Ops, SparseCore 0:
  20.8 32.0 all-reduce.2
  381.5 77.1 all-gather.1
  481.1 682.2 all-reduce.4
